TPU v7x, 32 devices: a whole 2x2x4 slice. The times are simulated.
32 devices in a mesh: grp: 2 (over y), seq: 4 (over z), head: 2 (over x), rep: 2 (over core).
Axes of the slice: x: 2, y: 2, z: 4, core: 2. Of those that a mesh axis runs over, the one named last changes fastest.
Arguments:
- tokens: bfloat16 [4096, 2048], P(('grp', 'seq'), 'rep'), parts along dimension 0, may hold values from -30 to 30, as said below
- projection: bfloat16 [2048, 3, 2048], P('rep', None, 'head'), may hold values from -0.116009706 to 0.116009706, as said below
- rand_table: int32 [16, 32, 3], P(('head', 'rep')), may hold values from 2 to 6
- round_masks: int32 [3], replicated, may hold values from 1 to 3, as said below
Outputs:
- context: bfloat16 [4096, 2048], P(('grp', 'seq'), ('head', 'rep')), parts along dimension 0
There are 2 independent parts, one for each index of `grp`. A program takes and returns all parts, laid end to end along the dimension named above; an argument that names none is the same for every part. Nothing has to cross between parts.
Inputs may be any that keep to these rules, and one draw needn't show every extreme that they name: `tokens`: floats of the inputs; a few rows may be larger than the rest. `projection`: query and key columns are scaled a little above the fan-in rule. 3 distinct values; in round r shard i is paired with shard i xor round_masks[r]; one of them is 3. `rand_table`: an entry names a block inside the partner shard, never its first two nor its last.
All inputs are finite; a program needn't handle non-finite values.
Results may differ from a plain program's by a relative error of at most 0.0011.
The roundings to bfloat16 on the way count: a program that leaves them out, or rounds other values in their place, can miss the bound.
Values may be sent and summed in bfloat16 or wider, within the bound.
A program may use at most 128 MiB of HBM per device.

v0:
```python
import functools

import jax
import jax.numpy as jnp
from jax import lax
from jax.experimental import pallas as pl
from jax.experimental.pallas import tpu as pltpu
from jax.sharding import PartitionSpec as P

HD = 128
B = 64
R = 3


def with_halo(block, sides, width):
    for axis, dim in sides:
        count = lax.axis_size(axis)
        forward = [(i, i + 1) for i in range(count - 1)]
        backward = [(target, source) for source, target in forward]
        low = lax.ppermute(
            lax.slice_in_dim(block, block.shape[dim] - width, None, axis=dim), axis, forward
        )
        high = lax.ppermute(lax.slice_in_dim(block, 0, width, axis=dim), axis, backward)
        block = jnp.concatenate([low, block, high], axis=dim)
    return block


def spread(shard, axis, root):
    mine = lax.axis_index(axis) == root
    return lax.psum(jnp.where(mine, shard, jnp.zeros_like(shard)), axis)


def from_partner(block, axis, apart):
    count = lax.axis_size(axis)
    route = []
    for low in range(count):
        high = low | 1 << apart
        if high != low and high < count:
            route += [(low, high), (high, low)]
    return lax.ppermute(block, axis, route)


def combined_all(part, axis, combine):
    gathered = jax.tree.map(lambda a: lax.all_gather(a, axis), part)

    def take(source):
        return jax.tree.map(lambda a: lax.dynamic_index_in_dim(a, source, 0, False), gathered)

    return lax.fori_loop(
        1, lax.axis_size(axis), lambda source, state: combine(state, take(source)), take(0)
    )


def combine_parts(former, latter):
    peak = jnp.maximum(former[0], latter[0])
    former_scale = jnp.exp(former[0] - peak)
    latter_scale = jnp.exp(latter[0] - peak)
    summed = former[1] * former_scale + latter[1] * latter_scale
    accum = former[2] * former_scale[..., None] + latter[2] * latter_scale[..., None]
    return (peak, summed, accum)


def take_blocks(source, indices):
    return jnp.take(source, indices, axis=1)


def bit_set(mask_value, bit_pos):
    return jnp.bitwise_and(jnp.right_shift(mask_value, bit_pos), 1) == 1


def body(tokens, projection, rand_table, round_masks):
    scale = HD ** (-0.5)
    tok_count = tokens.shape[0]
    width_local = tokens.shape[1]
    heads_group = projection.shape[2] // HD
    heads_here = heads_group // lax.axis_size("rep")
    blocks_here = tok_count // B
    shaped = projection.reshape(width_local, 3, heads_group, HD)
    summed = lax.psum_scatter(
        jnp.einsum("td,dshe->htse", tokens, shaped, preferred_element_type=jnp.float32),
        "rep",
        scatter_dimension=0,
        tiled=True,
    )
    mixed_rows = summed.astype(jnp.bfloat16)
    queries = mixed_rows[:, :, 0]
    key_vals = jnp.moveaxis(mixed_rows[:, :, 1:], 2, 0)
    shard_id = lax.axis_index("seq")
    shards = lax.axis_size("seq")
    total_blocks = shards * blocks_here
    padded = with_halo(key_vals, (("seq", 2),), B)
    window = jnp.stack(
        [
            padded[:, :, offset * B : offset * B + tok_count].reshape(
                2, heads_here, blocks_here, B, HD
            )
            for offset in range(3)
        ],
        axis=3,
    )
    window = window.reshape(2, heads_here, blocks_here, 3 * B, HD)
    lead_queries, lead_keys = (
        spread(queries[:, : 2 * B], "seq", 0),
        spread(key_vals[:, :, : 2 * B], "seq", 0),
    )
    global_part = jnp.broadcast_to(lead_keys[:, :, None], (2, heads_here, blocks_here, 2 * B, HD))
    blocked = key_vals.reshape(2, heads_here, blocks_here, B, HD)
    bit_count = shards.bit_length() - 1
    fetched = []
    for round_id in range(R):
        peer = jnp.bitwise_xor(shard_id, round_masks[round_id])
        wanted = lax.dynamic_slice_in_dim(
            rand_table[:, :, round_id], peer * blocks_here, blocks_here, 1
        )
        payload = jax.vmap(take_blocks, in_axes=(1, 0), out_axes=1)(blocked, wanted)
        for bit_pos in range(bit_count):
            swapped = from_partner(payload, "seq", bit_pos)
            payload = jnp.where(bit_set(round_masks[round_id], bit_pos), swapped, payload)
        fetched.append(payload)
    random_part = jnp.concatenate(fetched, axis=3)
    all_keys = jnp.concatenate([window, global_part, random_part], axis=3)
    block_ids = shard_id * blocks_here + jnp.arange(blocks_here, dtype=jnp.int32)
    nearby = block_ids[:, None] - 1 + jnp.arange(3, dtype=jnp.int32)[None, :]
    allowed = (nearby >= 2) & (nearby < total_blocks)
    allowed = jnp.repeat(allowed, B, axis=1)
    allowed = jnp.concatenate([allowed, jnp.ones((blocks_here, (2 + R) * B), dtype=bool)], axis=1)
    blocked_queries = queries.reshape(heads_here, blocks_here, B, HD)
    scores = (
        jnp.einsum(
            "hjqe,hjke->hjqk", blocked_queries, all_keys[0], preferred_element_type=jnp.float32
        )
        * scale
    )
    scores = jnp.where(allowed[None, :, None, :], scores, -jnp.inf)
    peak = jnp.max(scores, axis=-1, keepdims=True)
    expd = jnp.exp(scores - peak)
    row_total = jnp.sum(expd, axis=-1, keepdims=True)
    weights = expd.astype(jnp.bfloat16)
    regular = jnp.einsum(
        "hjqk,hjke->jqhe", weights, all_keys[1], preferred_element_type=jnp.float32
    )
    regular = regular / jnp.moveaxis(row_total, 0, 2)
    regular = regular.reshape(tok_count, heads_here, HD)
    gscores = (
        jnp.einsum("hqe,hke->hqk", lead_queries, key_vals[0], preferred_element_type=jnp.float32)
        * scale
    )
    local_peak = jnp.max(gscores, axis=-1)
    local_exp = jnp.exp(gscores - local_peak[..., None])
    local_sum = jnp.sum(local_exp, axis=-1)
    local_acc = jnp.einsum(
        "hqk,hke->hqe", local_exp, key_vals[1].astype(jnp.float32), precision=lax.Precision.HIGHEST
    )
    merged = combined_all((local_peak, local_sum, local_acc), "seq", combine_parts)
    global_rows = jnp.transpose(merged[2] / merged[1][..., None], (1, 0, 2))
    global_full = jnp.pad(global_rows, ((0, tok_count - 2 * B), (0, 0), (0, 0)))
    row_ids = jnp.arange(tok_count)
    use_global = (shard_id == 0) & (row_ids < 2 * B)
    combined = jnp.where(use_global[:, None, None], global_full, regular)
    return combined.reshape(tok_count, heads_here * HD).astype(jnp.bfloat16)


MESH = pl.DeviceIdType.MESH
DEPTH = 2 * B
OWNER = 0
X_LAG = 4
C_LAG = 7
CONTRACT = (((1,), (1,)), ((), ()))


def layer_kernel(
    shards, tok_ref, w_ref, q_s, k_s, v_s, full, wfull,
    zsend, zrecv, xsend, xrecv, csend, crecv, wsend, wrecv, lsem,
):
    s, x, c = lax.axis_index("seq"), lax.axis_index("head"), lax.axis_index("rep")
    rows, width = tok_ref.shape
    cols = width // 2
    mine = w_ref.shape[2] // 2
    heads = mine // HD
    blocks = rows // B
    steps = (shards - 1) * blocks
    has_up, has_down = s < shards - 1, s > 0
    up, down = {"seq": s + 1}, {"seq": s - 1}
    across, core = {"head": 1 - x}, {"rep": 1 - c}

    barrier = pltpu.get_barrier_semaphore()

    def greet(device):
        pl.semaphore_signal(barrier, inc=1, device_id=device, device_id_type=MESH)

    greet(across)
    greet(core)

    @pl.when(has_up)
    def _():
        greet(up)

    @pl.when(has_down)
    def _():
        greet(down)

    pl.semaphore_wait(barrier, 2 + has_up.astype(jnp.int32) + has_down.astype(jnp.int32))

    def remote(src, dst, send, recv, device):
        return pltpu.make_async_remote_copy(
            src_ref=src, dst_ref=dst, send_sem=send, recv_sem=recv, device_id=device, device_id_type=MESH
        )

    def rows_of(i, size=B):
        return pl.ds(pl.multiple_of(i * size, size), size)

    def quarter(i):
        return pl.ds(pl.multiple_of(c * width + i * cols, cols), cols)

    def half(i):
        return pl.ds(pl.multiple_of(i * width, width), width)

    def drawable(b):
        return (b >= 2) & (b < blocks - 1)

    def goes_up(at, src, b):
        return drawable(b) | ((b < 2) & (src == 0)) | ((b == blocks - 1) & (src == at))

    def goes_down(at, src, b):
        return drawable(b) | ((b == 0) & (src == at)) | (at > OWNER)

    def own_z(i, way):
        piece = tok_ref.at[rows_of(i), pl.ds(pl.multiple_of(x * cols, cols), cols)]
        return remote(piece, full.at[s, rows_of(i), quarter(x)], zsend.at[way, s, i], zrecv.at[s, i], (down, up)[way])

    def relay_z(src, i, way):
        piece = full.at[src, rows_of(i), quarter(x)]
        return remote(piece, piece, zsend.at[way, src, i], zrecv.at[src, i], (down, up)[way])

    def relay_x(src, i, which):
        piece = full.at[src, rows_of(i), quarter(which)]
        return remote(piece, piece, xsend.at[src, i], xrecv.at[src, i], across)

    def relay_c(src, i, which):
        piece = full.at[src, rows_of(i), half(which)]
        return remote(piece, piece, csend.at[src, i], crecv.at[src, i], core)

    def own_c(which):
        return remote(tok_ref, full.at[s, :, half(which)], wsend.at[3], wrecv.at[3], core)

    def weight_c(i, which):
        theirs = w_ref.at[i, :, pl.ds(pl.multiple_of((1 - c) * mine, mine), mine)]
        return remote(theirs, wfull.at[i, half(which), :], wsend.at[i], wrecv.at[i], core)

    def weight_l(i):
        own = w_ref.at[i, :, pl.ds(pl.multiple_of(c * mine, mine), mine)]
        return pltpu.make_async_copy(own, wfull.at[i, half(c), :], lsem.at[i])

    own_l = pltpu.make_async_copy(tok_ref, full.at[s, :, half(c)], lsem.at[3])

    def own_sends(act):
        def one(i, carry):
            @pl.when(has_up & goes_up(s, s, i))
            def _():
                act(own_z(i, 1))

            @pl.when(has_down & goes_down(s, s, i))
            def _():
                act(own_z(i, 0))

            return carry

        lax.fori_loop(0, blocks, one, 0)

    own_sends(lambda copy: copy.start())
    own_l.start()
    own_c(c).start()
    for i in (1, 2, 0):
        weight_c(i, c).start()
        weight_l(i).start()

    def product(src, pair, which):
        block = full[src, rows_of(pair, DEPTH), :]
        return jnp.dot(block, wfull[which], preferred_element_type=jnp.float32).astype(jnp.bfloat16)

    def put(dest, start, result):
        for h in range(heads):
            dest[h, pl.ds(pl.multiple_of(start, DEPTH), DEPTH), :] = result[:, h * HD:(h + 1) * HD]

    def project(src, pair):
        start = src * rows + pair * DEPTH
        put(k_s, start, product(src, pair, 1))
        put(v_s, start, product(src, pair, 2))

    def from_below(t, act):
        src, b = s - t // blocks - 1, t % blocks

        @pl.when((t >= 0) & (t < steps) & (src >= 0) & goes_up(s - 1, src, b))
        def _():
            act(src, b)

    def from_above(t, act):
        src, b = s + t // blocks + 1, t % blocks

        @pl.when((t >= 0) & (t < steps) & (src < shards) & goes_down(s + 1, src, b))
        def _():
            act(src, b)

    def pass_up(src, b, act):
        @pl.when(has_up & goes_up(s, src, b))
        def _():
            act(relay_z(src, b, 1))

    def pass_down(src, b, act):
        @pl.when(has_down & goes_down(s, src, b))
        def _():
            act(relay_z(src, b, 0))

    def take_z(passing):
        def act(src, b):
            relay_z(src, b, 0).wait_recv()
            passing(src, b, lambda copy: copy.start())
            relay_x(src, b, x).start()

        return act

    def take_x(src, b):
        relay_x(src, b, 1 - x).wait_recv()
        relay_c(src, b, c).start()

    def take_c(src, b):
        relay_c(src, b, 1 - c).wait_recv()

    def pairs(t):
        b = t % blocks
        whole = (t >= 0) & (t < steps) & (b % 2 == 1)
        low, high = s - t // blocks - 1, s + t // blocks + 1

        @pl.when(whole & (low >= 0) & ((b > 1) | (low == 0)))
        def _():
            project(low, b // 2)

        @pl.when(whole & (high < shards) & ((b > 1) | (high == s + 1) | (s >= OWNER)))
        def _():
            project(high, b // 2)

    def step(t, carry):
        from_below(t, take_z(pass_up))
        from_above(t, take_z(pass_down))
        from_below(t - X_LAG, take_x)
        from_above(t - X_LAG, take_x)

        @pl.when(t == 5)
        def _():
            own_l.wait()
            own_c(1 - c).wait_recv()
            for i in range(3):
                weight_l(i).wait()
                weight_c(i, 1 - c).wait_recv()

        @pl.when((t >= 5) & (t < 5 + blocks // 2))
        def _():
            project(s, t - 5)
            put(q_s, (t - 5) * DEPTH, product(s, t - 5, 0))

        from_below(t - C_LAG, take_c)
        from_above(t - C_LAG, take_c)
        pairs(t - C_LAG)
        return carry

    lax.fori_loop(0, steps + C_LAG, step, 0)

    own_c(c).wait_send()
    for i in range(3):
        weight_c(i, c).wait_send()
    own_sends(lambda copy: copy.wait_send())

    def sent(passing):
        def act(src, b):
            passing(src, b, lambda copy: copy.wait_send())
            relay_x(src, b, x).wait_send()
            relay_c(src, b, c).wait_send()

        return act

    def drain(t, carry):
        from_below(t, sent(pass_up))
        from_above(t, sent(pass_down))
        return carry

    lax.fori_loop(0, steps, drain, 0)


def attend_kernel(blocks, table_ref, mask_ref, q_ref, k_ref, v_ref, o_ref):
    h = pl.program_id(0)
    s = lax.axis_index("seq")
    total = k_ref.shape[1] // B
    scale = HD ** (-0.5)

    def rows_of(i):
        return pl.ds(pl.multiple_of(i * B, B), B)

    for j in range(blocks):
        g = s * blocks + j
        picks = [jnp.clip(g + d, 0, total - 1) for d in (-1, 0, 1)] + [0, 1]
        for r in range(R):
            peer = jnp.bitwise_xor(s, mask_ref[r])
            picks.append(peer * blocks + table_ref[r, h, g])
        keys = jnp.concatenate([k_ref[0, rows_of(p), :] for p in picks], axis=0)
        values = jnp.concatenate([v_ref[0, rows_of(p), :] for p in picks], axis=0)
        query = q_ref[0, j * B:(j + 1) * B, :]
        scores = lax.dot_general(query, keys, CONTRACT, preferred_element_type=jnp.float32) * scale
        col = lax.broadcasted_iota(jnp.int32, scores.shape, 1)
        near = g - 1 + col // B
        scores = jnp.where((col >= 3 * B) | ((near >= 2) & (near < total)), scores, -jnp.inf)
        expd = jnp.exp(scores - jnp.max(scores, axis=-1, keepdims=True))
        row_total = jnp.sum(expd, axis=-1, keepdims=True)
        out = jnp.dot(expd.astype(jnp.bfloat16), values, preferred_element_type=jnp.float32)
        o_ref[j * B:(j + 1) * B, :] = (out / row_total).astype(jnp.bfloat16)

    @pl.when(s == 0)
    def _():
        scores = lax.dot_general(q_ref[0, :DEPTH, :], k_ref[0], CONTRACT, preferred_element_type=jnp.float32) * scale
        expd = jnp.exp(scores - jnp.max(scores, axis=-1, keepdims=True))
        row_total = jnp.sum(expd, axis=-1, keepdims=True)
        high = expd.astype(jnp.bfloat16)
        low = (expd - high.astype(jnp.float32)).astype(jnp.bfloat16)
        values = v_ref[0]
        accum = jnp.dot(high, values, preferred_element_type=jnp.float32)
        accum += jnp.dot(low, values, preferred_element_type=jnp.float32)
        o_ref[:DEPTH, :] = (accum / row_total).astype(jnp.bfloat16)


def gathered_body(shards, tokens, projection, rand_table, round_masks):
    rows, width = tokens.shape
    mine = projection.shape[2] // 2
    heads = mine // HD
    blocks = rows // B
    dma = pltpu.SemaphoreType.DMA
    bf16 = jnp.bfloat16
    smem = pl.BlockSpec(memory_space=pltpu.SMEM)
    hbm = pl.BlockSpec(memory_space=pltpu.HBM)
    lengths = (rows, shards * rows, shards * rows)
    parts = pl.pallas_call(
        functools.partial(layer_kernel, shards),
        out_shape=tuple(jax.ShapeDtypeStruct((heads, length, HD), bf16) for length in lengths),
        in_specs=[hbm, hbm],
        out_specs=[pl.BlockSpec(memory_space=pltpu.VMEM)] * 3,
        scratch_shapes=[
            pltpu.VMEM((shards, rows, 2 * width), bf16),
            pltpu.VMEM((3, 2 * width, mine), bf16),
            dma((2, shards, blocks)),
            dma((shards, blocks)),
            dma((shards, blocks)),
            dma((shards, blocks)),
            dma((shards, blocks)),
            dma((shards, blocks)),
            dma((4,)),
            dma((4,)),
            dma((4,)),
        ],
        compiler_params=pltpu.CompilerParams(
            collective_id=0, has_side_effects=True, vmem_limit_bytes=48 * 1024 * 1024
        ),
        name="gather_project",
    )(tokens, jnp.transpose(projection, (1, 0, 2)))
    return pl.pallas_call(
        functools.partial(attend_kernel, blocks),
        out_shape=jax.ShapeDtypeStruct((rows, mine), bf16),
        grid=(heads,),
        in_specs=[smem, smem] + [pl.BlockSpec((1, length, HD), lambda h: (h, 0, 0)) for length in lengths],
        out_specs=pl.BlockSpec((rows, HD), lambda h: (0, h)),
        compiler_params=pltpu.CompilerParams(vmem_limit_bytes=12 * 1024 * 1024),
        name="attend",
    )(jnp.transpose(rand_table, (2, 0, 1)), round_masks, *parts)


def solution(mesh):
    shards = mesh.shape["seq"]
    few = shards == R + 1 and mesh.shape["head"] == 2
    return jax.shard_map(
        functools.partial(gathered_body, shards) if few else body,
        mesh=mesh,
        in_specs=(
            P(("grp", "seq"), "rep"),
            P("rep", None, "head"),
            P(("head", "rep"), None, None),
            P(),
        ),
        out_specs=P(("grp", "seq"), ("head", "rep")),
        check_vma=False,
    )
```

profile of v0, /device:TPU:0, one launch (start us, length us, event | category | flops | bytes accessed | tf_op | source)
XLA Modules:
  0.0 64.3 jit_solution(12431939881553701360)
XLA Ops:
  0.0 0.0 copy-start
  0.0 1.2 %copy-done = bf16[512,1024]{1,0:T(8,128)(2,1)S(1)} copy-done((bf16[512,1024]{1,0:T(8,128)(2,1)S(1)}, bf16[512,1024]{1,0:T(8,128)(2,1)}, u32[]{:S(2)}) %copy-start) | copy-done | bytes 1048600
  1.2 0.0 copy-start.1
  1.2 0.0 copy-start.2
  1.2 49.1 %gather_project.1 = (bf16[4,512,128]{2,1,0:T(8,128)(2,1)S(1)}, bf16[4,2048,128]{2,1,0:T(8,128)(2,1)S(1)}, bf16[4,2048,128]{2,1,0:T(8,128)(2,1)S(1)}) custom-call(bf16[512,1024]{1,0:T(8,128)(2,1)S(1)} %copy-done, bf16[3,1024,1024]{2,1,0:T(8,128)(2,1)} %bitcast.3), custom_call_target="tpu_custom_call" | custom-call | tf_op jit(solution)/shard_map/gather_project/pallas_call | solution.py:439
  50.4 0.0 copy-done.1
  50.4 0.0 copy-done.2
  50.4 13.9 %attend.1 = bf16[512,512]{1,0:T(8,128)(2,1)} custom-call(s32[3,4,32]{2,1,0:T(4,128)S(1)} %bitcast.2, s32[3]{0:T(128)S(1)} %copy-done.2, bf16[4,512,128]{2,1,0:T(8,128)(2,1)S(1)} %get-tuple-element.8.q_ref, bf16[4,2048,128]{2,1,0:T(8,128)(2,1)S(1)} %get-tuple-element.9.k_ref, bf16[4,2048,128]{2,1,0:T(8,128)(2,1)S(1)} %get-tuple-element.10.v_ref), custom_call_target="tpu_custom_call" | custom-call | tf_op jit(solution)/shard_map/attend/pallas_call | solution.py:462
Async XLA Ops:
  0.0 1.2 %copy-start = (bf16[512,1024]{1,0:T(8,128)(2,1)S(1)}, bf16[512,1024]{1,0:T(8,128)(2,1)}, u32[]{:S(2)}) copy-start(bf16[512,1024]{1,0:T(8,128)(2,1)} %tok_ref.1) | copy-start | bytes 3145732
  1.2 49.1 %copy-start.1 = (s32[4,32,3]{1,0,2:T(4,128)S(1)}, s32[4,32,3]{1,0,2:T(4,128)}, u32[]{:S(2)}) copy-start(s32[4,32,3]{1,0,2:T(4,128)} %param.6) | copy-start | bytes 4612
  1.2 49.2 %copy-start.2 = (s32[3]{0:T(128)S(1)}, s32[3]{0:T(128)}, u32[]{:S(2)}) copy-start(s32[3]{0:T(128)} %mask_ref.1) | copy-start | bytes 40
where the time goes:
time: 64.4 us; the launch traced here: 64.3 us
  Pallas kernels  63 us (98%)
  local copies, waits for them, and re-layouts  1.23 us (2%)
    pallas_call x1, Pallas kernels, gathered_body(): pl.pallas_call(functools.partial(layer_kernel, shards), out_shape=tuple((...  49.1 us
    pallas_call x1, Pallas kernels, gathered_body(): pl.pallas_call(functools.partial(attend_kernel, blocks), out_shape=jax.Sh...  13.9 us

commit v1 on v0

--- a/solution.py
+++ b/solution.py
@@ -165,6 +165,7 @@
 OWNER = 0
 X_LAG = 4
 C_LAG = 7
+LOG2E = 1.4426950408889634
 CONTRACT = (((1,), (1,)), ((), ()))
 
 
@@ -395,35 +396,51 @@
     def rows_of(i):
         return pl.ds(pl.multiple_of(i * B, B), B)
 
+    def picks(j):
+        g = s * blocks + j
+        chosen = [jnp.clip(g + d, 0, total - 1) for d in (-1, 0, 1)] + [0, 1]
+        for r in range(R):
+            chosen.append(jnp.bitwise_xor(s, mask_ref[r]) * blocks + table_ref[r, h, g])
+        return chosen
+
+    def taken(ref, j):
+        return jnp.concatenate([ref[0, rows_of(p), :] for p in picks(j)], axis=0)
+
+    def softmax(scores):
+        expd = jnp.exp2((scores - jnp.max(scores, axis=-1, keepdims=True)) * (scale * LOG2E))
+        return expd, 1.0 / jnp.sum(expd, axis=-1, keepdims=True)
+
+    lane = lax.broadcasted_iota(jnp.int32, (1, 2 * B), 1)
+    scores = [
+        lax.dot_general(q_ref[0, j * B:(j + 1) * B, :], taken(k_ref, j), CONTRACT, preferred_element_type=jnp.float32)
+        for j in range(blocks)
+    ]
+    weights, inverse = [], []
     for j in range(blocks):
-        g = s * blocks + j
-        picks = [jnp.clip(g + d, 0, total - 1) for d in (-1, 0, 1)] + [0, 1]
-        for r in range(R):
-            peer = jnp.bitwise_xor(s, mask_ref[r])
-            picks.append(peer * blocks + table_ref[r, h, g])
-        keys = jnp.concatenate([k_ref[0, rows_of(p), :] for p in picks], axis=0)
-        values = jnp.concatenate([v_ref[0, rows_of(p), :] for p in picks], axis=0)
-        query = q_ref[0, j * B:(j + 1) * B, :]
-        scores = lax.dot_general(query, keys, CONTRACT, preferred_element_type=jnp.float32) * scale
-        col = lax.broadcasted_iota(jnp.int32, scores.shape, 1)
-        near = g - 1 + col // B
-        scores = jnp.where((col >= 3 * B) | ((near >= 2) & (near < total)), scores, -jnp.inf)
-        expd = jnp.exp(scores - jnp.max(scores, axis=-1, keepdims=True))
-        row_total = jnp.sum(expd, axis=-1, keepdims=True)
-        out = jnp.dot(expd.astype(jnp.bfloat16), values, preferred_element_type=jnp.float32)
-        o_ref[j * B:(j + 1) * B, :] = (out / row_total).astype(jnp.bfloat16)
+        near = [s * blocks + j + d for d in (-1, 0, 1)]
+        below, here, above = [jnp.where((n >= 2) & (n < total), 0.0, -jnp.inf) for n in near]
+        masked = [
+            scores[j][:, :2 * B] + jnp.where(lane < B, below, here),
+            scores[j][:, 2 * B:4 * B] + jnp.where(lane < B, above, 0.0),
+            scores[j][:, 4 * B:],
+        ]
+        expd, over = softmax(jnp.concatenate(masked, axis=1))
+        weights.append(expd.astype(jnp.bfloat16))
+        inverse.append(over)
+    for j in range(blocks):
+        out = jnp.dot(weights[j], taken(v_ref, j), preferred_element_type=jnp.float32)
+        o_ref[j * B:(j + 1) * B, :] = (out * inverse[j]).astype(jnp.bfloat16)
 
     @pl.when(s == 0)
     def _():
-        scores = lax.dot_general(q_ref[0, :DEPTH, :], k_ref[0], CONTRACT, preferred_element_type=jnp.float32) * scale
-        expd = jnp.exp(scores - jnp.max(scores, axis=-1, keepdims=True))
-        row_total = jnp.sum(expd, axis=-1, keepdims=True)
+        scores = lax.dot_general(q_ref[0, :DEPTH, :], k_ref[0], CONTRACT, preferred_element_type=jnp.float32)
+        expd, over = softmax(scores)
         high = expd.astype(jnp.bfloat16)
         low = (expd - high.astype(jnp.float32)).astype(jnp.bfloat16)
         values = v_ref[0]
         accum = jnp.dot(high, values, preferred_element_type=jnp.float32)
         accum += jnp.dot(low, values, preferred_element_type=jnp.float32)
-        o_ref[:DEPTH, :] = (accum / row_total).astype(jnp.bfloat16)
+        o_ref[:DEPTH, :] = (accum * over).astype(jnp.bfloat16)
 
 
 def gathered_body(shards, tokens, projection, rand_table, round_masks):

time: 64.4 us -> 58.6 us (0.910)
  Pallas kernels: 63 us -> 57.2 us
    pallas_call x1, Pallas kernels: 13.9 us -> 8.04 us  [gathered_body(): pl.pallas_call(functools.partial(attend_kernel, blocks), out_shape=jax.Sh...]
where the time goes in v1:
time: 58.6 us; the launch traced here: 58.4 us
  Pallas kernels  57.2 us (98%)
  local copies, waits for them, and re-layouts  1.23 us (2%)
    pallas_call x1, Pallas kernels, gathered_body(): pl.pallas_call(functools.partial(layer_kernel, shards), out_shape=tuple((...  49.1 us
    pallas_call x1, Pallas kernels, gathered_body(): pl.pallas_call(functools.partial(attend_kernel, blocks), out_shape=jax.Sh...  8.04 us
    unnamed x6, local copies, waits for them, and re-layouts  1.23 us

profile of v1, /device:TPU:0, one launch (start us, length us, event | category | flops | bytes accessed | tf_op | source)
XLA Modules:
  0.0 58.4 jit_solution(94857687577757043)
XLA Ops:
  0.0 0.0 copy-start
  0.0 1.2 %copy-done = bf16[512,1024]{1,0:T(8,128)(2,1)S(1)} copy-done((bf16[512,1024]{1,0:T(8,128)(2,1)S(1)}, bf16[512,1024]{1,0:T(8,128)(2,1)}, u32[]{:S(2)}) %copy-start) | copy-done | bytes 1048600
  1.2 0.0 copy-start.1
  1.2 0.0 copy-start.2
  1.2 49.1 %gather_project.1 = (bf16[4,512,128]{2,1,0:T(8,128)(2,1)S(1)}, bf16[4,2048,128]{2,1,0:T(8,128)(2,1)S(1)}, bf16[4,2048,128]{2,1,0:T(8,128)(2,1)S(1)}) custom-call(bf16[512,1024]{1,0:T(8,128)(2,1)S(1)} %copy-done, bf16[3,1024,1024]{2,1,0:T(8,128)(2,1)} %bitcast.3), custom_call_target="tpu_custom_call" | custom-call | tf_op jit(solution)/shard_map/gather_project/pallas_call | solution.py:456
  50.4 0.0 copy-done.1
  50.4 0.0 copy-done.2
  50.4 8.0 %attend.1 = bf16[512,512]{1,0:T(8,128)(2,1)} custom-call(s32[3,4,32]{2,1,0:T(4,128)S(1)} %bitcast.2, s32[3]{0:T(128)S(1)} %copy-done.2, bf16[4,512,128]{2,1,0:T(8,128)(2,1)S(1)} %get-tuple-element.8.q_ref, bf16[4,2048,128]{2,1,0:T(8,128)(2,1)S(1)} %get-tuple-element.9.k_ref, bf16[4,2048,128]{2,1,0:T(8,128)(2,1)S(1)} %get-tuple-element.10.v_ref), custom_call_target="tpu_custom_call" | custom-call | tf_op jit(solution)/shard_map/attend/pallas_call | solution.py:479
Async XLA Ops:
  0.0 1.2 %copy-start = (bf16[512,1024]{1,0:T(8,128)(2,1)S(1)}, bf16[512,1024]{1,0:T(8,128)(2,1)}, u32[]{:S(2)}) copy-start(bf16[512,1024]{1,0:T(8,128)(2,1)} %tok_ref.1) | copy-start | bytes 3145732
  1.2 49.1 %copy-start.1 = (s32[4,32,3]{1,0,2:T(4,128)S(1)}, s32[4,32,3]{1,0,2:T(4,128)}, u32[]{:S(2)}) copy-start(s32[4,32,3]{1,0,2:T(4,128)} %param.6) | copy-start | bytes 4612
  1.2 49.2 %copy-start.2 = (s32[3]{0:T(128)S(1)}, s32[3]{0:T(128)}, u32[]{:S(2)}) copy-start(s32[3]{0:T(128)} %mask_ref.1) | copy-start | bytes 40
